TPU v7x, 32 devices: a whole 2x2x4 slice. The times are simulated.
32 devices in a mesh: prow: 4 (over y, x), pcol: 8 (over z, core).
Axes of the slice: x: 2, y: 2, z: 4, core: 2. Of those that a mesh axis runs over, the one named last changes fastest.
Arguments:
- matrix: float32 [2048, 1024], P('prow', 'pcol'), may hold values from -6 to 6
- panel: float32 [2048, 1024], P(('prow', 'pcol')), as said below
- pivots: int32 [1024], replicated, may hold values from 0 to 2047, as said below
Outputs:
- trailing: float32 [2048, 1024], P('prow', 'pcol')
Inputs may be any that keep to these rules, and one draw needn't show every extreme that they name: pivots[i] is either i itself or a row at or beyond 1024; the rows at or beyond 1024 that are named are all different; at most 264 of them lie in the rows of one index of prow, and some index of prow holds exactly 264. `panel`: the top 1024 rows are unit lower triangular.
All inputs are finite; a program needn't handle non-finite values.
Results may differ from a plain program's by a relative error of at most 0.000061.
Values sent between devices are 32-bit elements; how exact they have to be, the bound alone decides.
No kernel may reach another device: no remote copies, remote signals or barrier semaphores. Data moves between devices by JAX's collectives and lax.ppermute only.
A program may use at most 64 MiB of HBM per device.

v0:
```python
import jax
import jax.numpy as jnp
from jax import lax
from jax.sharding import PartitionSpec as P


def spread(block, axis, holder):
    block = jnp.where(lax.axis_index(axis) == holder, block, jnp.zeros_like(block))
    return lax.psum(block, axis)


def per_device(matrix, panel, pivots):
    rows, cols = matrix.shape
    block = pivots.shape[0]
    first = lax.axis_index("prow") * rows
    local_pivot = pivots - first
    owned = (local_pivot >= 0) & (local_pivot < rows)
    picked = jnp.take(matrix, jnp.clip(local_pivot, 0, rows - 1), axis=0)
    picked = jnp.where(owned[:, None], picked, 0.0)
    panel_block = lax.all_gather(panel, "pcol", axis=0, tiled=True)
    shares = lax.psum_scatter(picked, "prow", scatter_dimension=0, tiled=True)
    solved = jnp.dot(
        panel_block,
        lax.all_gather(shares, "prow", axis=0, tiled=True),
        precision=lax.Precision.HIGHEST,
        preferred_element_type=jnp.float32,
    )
    rows_here = first + jnp.arange(rows, dtype=jnp.int32)
    match = pivots[None, :] == rows_here[:, None]
    moved = jnp.any(match, axis=1) & (rows_here >= block)
    source = jnp.sum(jnp.where(match, jnp.arange(block, dtype=jnp.int32)[None, :], 0), axis=1)
    upper = jnp.zeros((block, cols), jnp.float32)
    top_old = jnp.zeros((block, cols), jnp.float32)
    for root in range(block // rows):
        piece_u, old_rows = (spread(solved, "prow", root), spread(matrix, "prow", root))
        upper = lax.dynamic_update_slice_in_dim(upper, piece_u, root * rows, 0)
        top_old = lax.dynamic_update_slice_in_dim(top_old, old_rows, root * rows, 0)
    replaced = jnp.take(top_old, source, axis=0)
    permuted = jnp.where(moved[:, None], replaced, matrix)
    lower = permuted - jnp.dot(
        panel_block, upper, precision=lax.Precision.HIGHEST, preferred_element_type=jnp.float32
    )
    return jnp.where((rows_here < block)[:, None], solved, lower)


def solution(mesh):
    placed = (P("prow", "pcol"), P(("prow", "pcol"), None), P())
    return jax.shard_map(
        per_device, mesh=mesh, in_specs=placed, out_specs=P("prow", "pcol"), check_vma=False
    )
```

profile of v0, /device:TPU:0, one launch (start us, length us, event | category | flops | bytes accessed | tf_op | source)
XLA Modules:
  0.0 123.5 jit_solution(4456176629479633744)
XLA Ops:
  7.4 0.7 fusion.6
  8.1 0.7 compare_and_fusion.1
  8.8 3.8 %gather_fusion = f32[1024,128]{1,0:T(8,128)S(1)} fusion(f32[512,128]{1,0:T(8,128)} %param.3, s32[1024]{0:T(1024)S(1)} %fusion.6), kind=kCustom, calls=%fused_computation | custom fusion | bytes 1052672 | tf_op jit(solution)/shard_map/jit(_take)/gather | solution.py:18
  12.6 1.1 select_select_fusion
  13.8 0.0 all-gather.2.cloned.1.call-start
  13.8 0.5 all-gather.2.cloned.1.call-update
  14.3 0.0 all-reduce.3.cloned.1.call-start
  14.4 0.1 copy.16
  14.5 0.9 broadcast_select_fusion.3
  15.4 26.3 %reduce-scatter.2.cloned.1.call-done = f32[256,128]{1,0:T(8,128)} async-done(((f32[1024,128]{1,0:T(8,128)}), f32[256,128]{1,0:T(8,128)}) %reduce-scatter.2.cloned.1.call-update) | async-done | bytes 131088 | tf_op jit(solution)/shard_map/reduce_scatter | solution.py:21
  41.7 10.0 %all_gather.6 = f32[1024,128]{1,0:T(8,128)S(1)} all-gather(f32[256,128]{1,0:T(8,128)} %reduce-scatter.2.cloned.1.call-done), channel_id=1, replica_groups=mesh['prow'=4,'pcol'=8] {'prow'}, dimensions={0}, use_global_device_ids=true | all-gather | bytes 655360 | tf_op jit(solution)/shard_map/all_gather | solution.py:24
  51.7 0.0 all-gather.2.cloned.1.call-done
  51.8 4.8 %broadcast_select_fusion.1 = (f32[512,128]{0,1:T(8,128)}, f32[512,128]{0,1:T(8,128)}, f32[512,128]{0,1:T(8,128)}) fusion(pred[]{:T(512)S(6)} %eq.24, pred[]{:T(512)S(6)} %eq.25, f32[1024,128]{1,0:T(8,128)S(1)} %all_gather.6, f32[512,1024]{1,0:T(8,128)} %all-gather.2.cloned.1.call-done), kind=kOutput, calls=%fused_computation.15 | convolution fusion | flops 805437440 | bytes 3407874 | tf_op jit(solution)/shard_map/dot_general | solution.py:22
  56.6 0.4 fusion
  57.0 0.4 compare_reduce_fusion
  57.4 51.8 %all-reduce.3.cloned.1.call-done = (f32[512,128]{0,1:T(8,128)}, f32[512,128]{0,1:T(8,128)}, f32[512,128]{0,1:T(8,128)}, f32[512,128]{0,1:T(8,128)}) async-done(((f32[512,128]{0,1:T(8,128)}, f32[512,128]{0,1:T(8,128)}, f32[512,128]{0,1:T(8,128)}, f32[512,128]{0,1:T(8,128)}), (f32[512,128]{0,1:T(8,128)}, f32[512,128]{0,1:T(8,128)}, f32[512,128]{0,1:T(8,128)}, ...) | async-done | bytes 1048592 | tf_op jit(solution)/shard_map/psum | solution.py:9
  109.3 1.1 pad_maximum_fusion
  110.3 0.2 copy.18
  110.5 1.0 gather_fusion.1
  111.6 0.1 copy.19
  111.7 0.2 copy-done.1
  111.9 0.0 copy-done.2
  111.9 3.3 %fusion.2 = f32[512,128]{0,1:T(8,128)S(1)} fusion(f32[512,128]{0,1:T(8,128)S(1)} %copy-done.2, f32[512,1024]{1,0:T(8,128)S(1)} %copy-done.1, f32[512,128]{0,1:T(8,128)} %get-tuple-element.5, f32[512,128]{0,1:T(8,128)} %get-tuple-element.6, f32[512,128]{0,1:T(8,128)S(1)} %copy.16, f32[512,128]{0,1:T(8,128)S(1)} %copy.19, ...), kind=kOutput, calls=%fused_computation.8 | convolution fusion | flops 805699584 | bytes 3671552 | tf_op jit(solution)/shard_map/dot_general | solution.py:40
  115.2 0.8 copy.21
  (14 shorter events, 0.1 us)
Async XLA Ops:
  7.4 34.4 %reduce-scatter.2.cloned.1.call-start = ((), (), s32[]{:S(2)}) async-start(), calls=%async_computation.1 | async-start | bytes 655360 | tf_op jit(solution)/shard_map/reduce_scatter | solution.py:21
  8.8 5.6 %copy-start = (f32[512,128]{1,0:T(8,128)S(1)}, f32[512,128]{1,0:T(8,128)}, u32[]{:S(2)}) copy-start(f32[512,128]{1,0:T(8,128)} %param.3) | copy-start | bytes 786436
  13.8 38.0 %all-gather.2.cloned.1.call-start = ((), (), s32[]{:S(2)}) async-start(), calls=%async_computation.2 | async-start | bytes 2359296 | tf_op jit(solution)/shard_map/all_gather | solution.py:20
  14.3 94.9 %all-reduce.3.cloned.1.call-start = ((), (), s32[]{:S(2)}) async-start(), calls=%async_computation.3 | async-start | bytes 2097152 | tf_op jit(solution)/shard_map/psum | solution.py:9
  51.7 4.9 %copy-start.3 = (s32[1024]{0:T(1024)S(1)}, s32[1024]{0:T(1024)}, u32[]{:S(2)}) copy-start(s32[1024]{0:T(1024)} %param.5) | copy-start | bytes 12292
  110.3 1.6 %copy-start.1 = (f32[512,1024]{1,0:T(8,128)S(1)}, f32[512,1024]{1,0:T(8,128)}, u32[]{:S(2)}) copy-start(f32[512,1024]{1,0:T(8,128)} %all-gather.2.cloned.1.call-done) | copy-start | bytes 6291460
  110.5 1.4 %copy-start.2 = (f32[512,128]{0,1:T(8,128)S(1)}, f32[512,128]{0,1:T(8,128)}, u32[]{:S(2)}) copy-start(f32[512,128]{0,1:T(8,128)} %get-tuple-element.15) | copy-start | bytes 786436
Sparse Core Ops, SparseCore 0:
  13.9 27.8 reduce-scatter.1
  56.7 52.5 all-reduce.2
Sparse Core Ops, SparseCore 1:
  15.8 31.8 all-gather.1
where the time goes:
time: 124 us; the launch traced here: 123 us
  waiting for transfers between devices  78.7 us (63%)
  between operations  15 us (12%)
  blocking collectives  9.99 us (8%)
  matrix products  8.06 us (6%)
  local copies, waits for them, and re-layouts  6.37 us (5%)
  other arithmetic  5.29 us (4%)
    psum x1, waiting for transfers between devices, spread(): return lax.psum(block, axis)  51.8 us
    reduce_scatter x1, waiting for transfers between devices, per_device(): shares = lax.psum_scatter(picked, 'prow', scatter_dimension=0, tiled=True)  26.3 us
    all_gather x1, blocking collectives, per_device(): lax.all_gather(shares, 'prow', axis=0, tiled=True)  9.99 us
    dot_general x1, matrix products, per_device(): jnp.dot(panel_block, lax.all_gather(shares, 'prow', axis=0, tiled=True),...  4.79 us
    gather x1, local copies, waits for them, and re-layouts, per_device(): picked = jnp.take(matrix, jnp.clip(local_pivot, 0, rows - 1), axis=0)  3.82 us
    dot_general x1, matrix products, per_device(): jnp.dot(panel_block, upper, precision=lax.Precision.HIGHEST, preferred_el...  3.28 us
  transfers between devices with their start and end apart: 3, of which 2 were waited for; matrix products, arithmetic and copies ran while one was open for 1% of the time, Pallas kernels for 0%

commit v1 on v0

--- a/solution.py
+++ b/solution.py
@@ -6,7 +6,7 @@
 
 def spread(block, axis, holder):
     block = jnp.where(lax.axis_index(axis) == holder, block, jnp.zeros_like(block))
-    return lax.psum(block, axis)
+    return jnp.sum(lax.all_gather(block, axis), axis=0)
 
 
 def per_device(matrix, panel, pivots):

time: 124 us -> 175 us (1.41)
  waiting for transfers between devices: 78.7 us -> 118 us
  local copies, waits for them, and re-layouts: 6.37 us -> 14.7 us
  other arithmetic: 5.29 us -> 8.16 us
    all_gather x0 -> x4, waiting for transfers between devices: none -> 91 us  [spread(): return jnp.sum(lax.all_gather(block, axis), axis=0)]
    psum x1 -> x0, waiting for transfers between devices: 51.8 us -> none  [spread(): return lax.psum(block, axis)]
    all_gather x0 -> x4, local copies, waits for them, and re-layouts: none -> 7.73 us  [spread(): return jnp.sum(lax.all_gather(block, axis), axis=0)]
    reduce_sum x0 -> x4, other arithmetic: none -> 3.91 us  [spread(): return jnp.sum(lax.all_gather(block, axis), axis=0)]
  transfers between devices with their start and end apart: 3 -> 6, of which waited for: 2 -> 5; matrix products, arithmetic and copies ran while one was open for 1% -> 10% of each run, Pallas kernels for 0% -> 0%
where the time goes in v1:
time: 175 us
  waiting for transfers between devices  118 us (67%)
  between operations  15.2 us (9%)
  local copies, waits for them, and re-layouts  14.7 us (8%)
  blocking collectives  9.99 us (6%)
  matrix products  8.24 us (5%)
  other arithmetic  8.16 us (5%)
    all_gather x4, waiting for transfers between devices, spread(): return jnp.sum(lax.all_gather(block, axis), axis=0)  91 us
    reduce_scatter x1, waiting for transfers between devices, per_device(): shares = lax.psum_scatter(picked, 'prow', scatter_dimension=0, tiled=True)  25.7 us
    all_gather x1, blocking collectives, per_device(): lax.all_gather(shares, 'prow', axis=0, tiled=True)  9.99 us
    all_gather x4, local copies, waits for them, and re-layouts, spread(): return jnp.sum(lax.all_gather(block, axis), axis=0)  7.73 us
    dot_general x1, matrix products, per_device(): jnp.dot(panel_block, lax.all_gather(shares, 'prow', axis=0, tiled=True),...  4.81 us
    reduce_sum x4, other arithmetic, spread(): return jnp.sum(lax.all_gather(block, axis), axis=0)  3.91 us
    gather x1, local copies, waits for them, and re-layouts, per_device(): picked = jnp.take(matrix, jnp.clip(local_pivot, 0, rows - 1), axis=0)  3.82 us
  transfers between devices with their start and end apart: 6, of which 5 were waited for; matrix products, arithmetic and copies ran while one was open for 10% of the time, Pallas kernels for 0%

profile of v1, /device:TPU:0, one launch (start us, length us, event | category | flops | bytes accessed | tf_op | source)
XLA Modules:
  0.0 175.0 jit_solution(6339947585957251605)
XLA Ops:
  7.4 0.7 compare_and_fusion.1
  8.1 0.7 fusion.6
  8.8 3.8 %gather_fusion = f32[1024,128]{1,0:T(8,128)S(1)} fusion(f32[512,128]{1,0:T(8,128)} %param.3, s32[1024]{0:T(1024)S(1)} %fusion.6), kind=kCustom, calls=%fused_computation | custom fusion | bytes 1052672 | tf_op jit(solution)/shard_map/jit(_take)/gather | solution.py:18
  12.6 1.1 select_select_fusion
  14.5 0.9 broadcast_select_fusion.3
  16.1 25.7 %reduce-scatter.2.cloned.1.call-done = f32[256,128]{1,0:T(8,128)} async-done(((f32[1024,128]{1,0:T(8,128)}), f32[256,128]{1,0:T(8,128)}) %reduce-scatter.2.cloned.1.call-update) | async-done | bytes 131088 | tf_op jit(solution)/shard_map/reduce_scatter | solution.py:21
  41.7 10.0 %all_gather.30 = f32[1024,128]{1,0:T(8,128)S(1)} all-gather(f32[256,128]{1,0:T(8,128)} %reduce-scatter.2.cloned.1.call-done), channel_id=1, replica_groups=mesh['prow'=4,'pcol'=8] {'prow'}, dimensions={0}, use_global_device_ids=true | all-gather | bytes 655360 | tf_op jit(solution)/shard_map/all_gather | solution.py:24
  51.8 4.8 %broadcast_select_fusion.1 = (f32[512,128]{0,1:T(8,128)}, f32[512,128]{0,1:T(8,128)}, f32[512,128]{0,1:T(8,128)}) fusion(pred[]{:T(512)S(6)} %eq.24, pred[]{:T(512)S(6)} %eq.25, f32[1024,128]{1,0:T(8,128)S(1)} %all_gather.30, f32[512,1024]{1,0:T(8,128)} %all-gather.10.cloned.1.call-done), kind=kOutput, calls=%fused_computation.15 | convolution fusion | flops 805437440 | bytes 3407874 | tf_op jit(solution)/shard_map/dot_general | solution.py:22
  58.2 16.9 %all-gather.12.cloned.1.call-done = f32[2048,128]{0,1:T(8,128)} async-done(((f32[512,128]{0,1:T(8,128)}), f32[2048,128]{0,1:T(8,128)}) %all-gather.12.cloned.1.call-update) | async-done | bytes 1048592 | tf_op jit(solution)/shard_map/all_gather | solution.py:9
  75.2 1.9 %reshape.54 = f32[4,512,128]{1,0,2:T(4,128)S(1)} reshape(f32[2048,128]{0,1:T(8,128)} %all-gather.12.cloned.1.call-done) | data formatting | bytes 2097152 | tf_op jit(solution)/shard_map/all_gather | solution.py:9
  77.1 0.6 reduce_sum.48
  77.9 25.4 %all-gather.14.cloned.1.call-done = f32[2048,128]{0,1:T(8,128)} async-done(((f32[512,128]{0,1:T(8,128)}), f32[2048,128]{0,1:T(8,128)}) %all-gather.14.cloned.1.call-update) | async-done | bytes 1048592 | tf_op jit(solution)/shard_map/all_gather | solution.py:9
  103.3 1.9 %reshape.55 = f32[4,512,128]{1,0,2:T(4,128)S(1)} reshape(f32[2048,128]{0,1:T(8,128)} %all-gather.14.cloned.1.call-done) | data formatting | bytes 2097152 | tf_op jit(solution)/shard_map/all_gather | solution.py:9
  105.2 0.6 reduce_sum.49
  106.0 1.0 gather_fusion.1
  107.1 0.9 copy.25
  107.9 23.6 %all-gather.16.cloned.1.call-done = f32[2048,128]{0,1:T(8,128)} async-done(((f32[512,128]{0,1:T(8,128)}), f32[2048,128]{0,1:T(8,128)}) %all-gather.16.cloned.1.call-update) | async-done | bytes 1048592 | tf_op jit(solution)/shard_map/all_gather | solution.py:9
  131.6 1.9 %reshape.56 = f32[4,512,128]{1,0,2:T(4,128)S(1)} reshape(f32[2048,128]{0,1:T(8,128)} %all-gather.16.cloned.1.call-done) | data formatting | bytes 2097152 | tf_op jit(solution)/shard_map/all_gather | solution.py:9
  133.5 1.3 reduce_sum.51
  134.8 25.0 %all-gather.18.cloned.1.call-done = f32[2048,128]{0,1:T(8,128)} async-done(((f32[512,128]{0,1:T(8,128)}), f32[2048,128]{0,1:T(8,128)}) %all-gather.18.cloned.1.call-update) | async-done | bytes 1048592 | tf_op jit(solution)/shard_map/all_gather | solution.py:9
  159.8 1.9 %reshape.57 = f32[4,512,128]{1,0,2:T(4,128)S(1)} reshape(f32[2048,128]{0,1:T(8,128)} %all-gather.18.cloned.1.call-done) | data formatting | bytes 2097152 | tf_op jit(solution)/shard_map/all_gather | solution.py:9
  161.8 1.3 reduce_sum.52
  163.1 3.4 %fusion.2 = f32[512,128]{0,1:T(8,128)S(1)} fusion(f32[512,128]{0,1:T(8,128)} %get-tuple-element.11, f32[512,1024]{1,0:T(8,128)S(1)} %copy-done.1, f32[512,128]{0,1:T(8,128)} %reduce_sum.52, f32[512,128]{0,1:T(8,128)} %reduce_sum.51, f32[512,128]{0,1:T(8,128)S(1)} %copy.21, f32[512,128]{0,1:T(8,128)} %copy.25, pred[512]{0:T(512)(128)(4,1)S(1)} %compare_and_fusion.2, ...), kind=kOutput, calls=%fused_computation.8 | convolution fusion | flops 805699584 | bytes 3671552 | tf_op jit(solution)/shard_map/dot_general | solution.py:40
  166.6 0.8 copy.27
  (31 shorter events, 3.3 us)
Async XLA Ops:
  7.4 34.4 %reduce-scatter.2.cloned.1.call-start = ((), (), s32[]{:S(2)}) async-start(), calls=%async_computation.1 | async-start | bytes 655360 | tf_op jit(solution)/shard_map/reduce_scatter | solution.py:21
  8.8 5.6 %copy-start = (f32[512,128]{1,0:T(8,128)S(1)}, f32[512,128]{1,0:T(8,128)}, u32[]{:S(2)}) copy-start(f32[512,128]{1,0:T(8,128)} %param.3) | copy-start | bytes 786436
  13.8 38.0 %all-gather.10.cloned.1.call-start = ((), (), s32[]{:S(2)}) async-start(), calls=%async_computation.2 | async-start | bytes 2359296 | tf_op jit(solution)/shard_map/all_gather | solution.py:20
  14.3 60.8 %all-gather.12.cloned.1.call-start = ((), (), s32[]{:S(2)}) async-start(), calls=%async_computation.3 | async-start | bytes 1310720 | tf_op jit(solution)/shard_map/all_gather | solution.py:9
  15.4 87.9 %all-gather.14.cloned.1.call-start = ((), (), s32[]{:S(2)}) async-start(), calls=%async_computation.4 | async-start | bytes 1310720 | tf_op jit(solution)/shard_map/all_gather | solution.py:9
  16.0 115.6 %all-gather.16.cloned.1.call-start = ((), (), s32[]{:S(2)}) async-start(), calls=%async_computation.5 | async-start | bytes 1310720 | tf_op jit(solution)/shard_map/all_gather | solution.py:9
  51.7 5.6 %copy-start.2 = (s32[1024]{0:T(1024)S(1)}, s32[1024]{0:T(1024)}, u32[]{:S(2)}) copy-start(s32[1024]{0:T(1024)} %param.5) | copy-start | bytes 12292
  56.6 103.3 %all-gather.18.cloned.1.call-start = ((), (), s32[]{:S(2)}) async-start(), calls=%async_computation.6 | async-start | bytes 1310720 | tf_op jit(solution)/shard_map/all_gather | solution.py:9
  133.5 29.6 %copy-start.1 = (f32[512,1024]{1,0:T(8,128)S(1)}, f32[512,1024]{1,0:T(8,128)}, u32[]{:S(2)}) copy-start(f32[512,1024]{1,0:T(8,128)} %all-gather.10.cloned.1.call-done) | copy-start | bytes 6291460
Sparse Core Ops, SparseCore 0:
  13.9 27.8 reduce-scatter.1
Sparse Core Ops, SparseCore 1:
  15.8 31.8 all-gather.9
  49.4 25.7 all-gather.11
  76.9 26.3 all-gather.13
  105.2 26.3 all-gather.15
  133.4 26.3 all-gather.17
